TPU v7x, 32 devices: a whole 2x2x4 slice. The times are simulated.
32 devices in a mesh: parts: 2 (over y), off: 4 (over z), depth: 2 (over x), shot: 2 (over core).
Axes of the slice: x: 2, y: 2, z: 4, core: 2. Of those that a mesh axis runs over, the one named last changes fastest.
Arguments:
- image: bfloat16 [64, 32, 32, 256], P('off', None, 'depth'), may hold values from -4 to 4
- offset_of: int32 [64], P('off'), may hold values from 0 to 63, each once
- background: bfloat16 [4, 32, 32, 256], P(('parts', 'shot'), 'off', 'depth'), parts along dimension 0, may hold values from -6 to 6
- wave_now: float32 [4, 32, 32, 256], P(('parts', 'shot'), 'off', 'depth'), parts along dimension 0, may hold values from -6 to 6
- wave_prev: float32 [4, 32, 32, 256], P(('parts', 'shot'), 'off', 'depth'), parts along dimension 0, may hold values from -6 to 6
- courant: float32 [32, 32, 256], P('off', 'depth'), may hold values from 0.02 to 0.15
Outputs:
- wave_next: float32 [4, 32, 32, 256], P(('parts', 'shot'), 'off', 'depth'), parts along dimension 0
There are 2 independent parts, one for each index of `parts`. A program takes and returns all parts, laid end to end along the dimension named above; an argument that names none is the same for every part. Nothing has to cross between parts.
Inputs may be any that keep to these rules, and one draw needn't show every extreme that they name: Each value appears once; image column k holds offset offset_of[k] - 32 cells along x.
All inputs are finite; a program needn't handle non-finite values.
Results may differ from a plain program's by a relative error of at most 0.0003.
Values may be sent and summed in bfloat16 or wider, within the bound.
A program may use at most 64 MiB of HBM per device.

v0:
```python
import jax
import jax.numpy as jnp
from jax import lax
from jax.sharding import PartitionSpec as P

H = 64
STENCIL = (-205.0 / 72.0, 8.0 / 5.0, -1.0 / 5.0, 8.0 / 315.0, -1.0 / 560.0)


def extended_2(cells, sides, width):
    for axis, dim in sides:
        count = lax.axis_size(axis)
        ends = count - 1
        head = lax.slice_in_dim(cells, 0, width, axis=dim)
        tail = lax.slice_in_dim(cells, cells.shape[dim] - width, cells.shape[dim], axis=dim)
        cells = jnp.concatenate(
            [
                lax.ppermute(tail, axis, [(i, (i + 1) % count) for i in range(ends)]),
                cells,
                lax.ppermute(head, axis, [((i + 1) % count, i) for i in range(ends)]),
            ],
            axis=dim,
        )
    return cells


def laplace(padded, rows_y, rows_z, cols_x):
    extended = jnp.pad(padded, ((0, 0), (0, 0), (4, 4)))
    centre = extended[4 : 4 + rows_y, 4 : 4 + rows_z, 4 : 4 + cols_x]
    running = 3.0 * STENCIL[0] * centre
    for radius in range(1, 5):
        beside_all = extended[4 + radius : 4 + radius + rows_y, 4 : 4 + rows_z, 4 : 4 + cols_x]
        beside_all = (
            beside_all + extended[4 - radius : 4 - radius + rows_y, 4 : 4 + rows_z, 4 : 4 + cols_x]
        )
        beside_all = (
            beside_all + extended[4 : 4 + rows_y, 4 + radius : 4 + radius + rows_z, 4 : 4 + cols_x]
        )
        beside_all = (
            beside_all + extended[4 : 4 + rows_y, 4 - radius : 4 - radius + rows_z, 4 : 4 + cols_x]
        )
        beside_all = (
            beside_all + extended[4 : 4 + rows_y, 4 : 4 + rows_z, 4 + radius : 4 + radius + cols_x]
        )
        beside_all = (
            beside_all + extended[4 : 4 + rows_y, 4 : 4 + rows_z, 4 - radius : 4 - radius + cols_x]
        )
        running = running + STENCIL[radius] * beside_all
    return running


def on_device(image, offset_of, background, wave_now, wave_prev, courant):
    slab_rows = wave_now.shape[1]
    depth_rows = wave_now.shape[2]
    width_x = wave_now.shape[3]
    local_cols = image.shape[0]
    half_span = H // 2
    gathered = lax.all_gather(background, "off", axis=1, tiled=True)
    extended_bg = jnp.pad(gathered[0], ((0, 0), (0, 0), (half_span, half_span)))
    first_index = jnp.asarray(jnp.int32(0), jnp.int32)

    def add_column(column, running):
        offset_cells = offset_of[column] - half_span
        whole_col = lax.dynamic_index_in_dim(image, column, 0, keepdims=False)
        starts = (first_index, jnp.zeros((), jnp.int32), half_span - offset_cells)
        shifted = lax.dynamic_slice(
            extended_bg, starts, (slab_rows * lax.axis_size("off"), depth_rows, width_x)
        )
        return running + whole_col.astype(jnp.float32) * shifted.astype(jnp.float32)

    own_source = lax.psum_scatter(
        lax.fori_loop(
            0,
            local_cols,
            add_column,
            jnp.zeros((slab_rows * lax.axis_size("off"), depth_rows, width_x), jnp.float32),
        ),
        "off",
        scatter_dimension=0,
        tiled=True,
    )
    padded = extended_2(wave_now[0], (("off", 0), ("depth", 1)), 4)
    bending = laplace(padded, slab_rows, depth_rows, width_x)
    stepped = 2.0 * wave_now[0] - wave_prev[0] + courant * (bending + own_source)
    return stepped[None]


def solution(mesh):
    return jax.shard_map(
        on_device,
        mesh=mesh,
        in_specs=(
            P("off", None, "depth", None),
            P("off"),
            P(("parts", "shot"), "off", "depth", None),
            P(("parts", "shot"), "off", "depth", None),
            P(("parts", "shot"), "off", "depth", None),
            P("off", "depth", None),
        ),
        out_specs=P(("parts", "shot"), "off", "depth", None),
        check_vma=False,
    )
```

profile of v0, /device:TPU:0, one launch (start us, length us, event | category | flops | bytes accessed | tf_op | source)
XLA Modules:
  0.0 105.7 jit_solution(5302099178217128605)
XLA Ops:
  6.5 15.9 %all_gather.3 = bf16[1,32,16,256]{3,2,0,1:T(8,128)(2,1)S(1)} all-gather(bf16[1,8,16,256]{3,2,0,1:T(8,128)(2,1)} %bitcast.29), channel_id=1, replica_groups=mesh['parts'=2,'off'=4,'depth'=2,'shot'=2] {'off'}, dimensions={1}, use_global_device_ids=true | all-gather | bytes 327680 | tf_op jit(solution)/shard_map/all_gather | solution.py:58
  22.6 50.0 %while.16 = (s32[]{:T(128)}, f32[32,16,256]{2,1,0:T(8,128)S(1)}, bf16[16,32,16,256]{3,2,1,0:T(8,128)(2,1)}, s32[16]{0:T(128)}, bf16[32,16,320]{2,1,0:T(8,128)(2,...) while((s32[]{:T(128)}, f32[32,16,256]{2,1,0:T(8,128)S(1)}, ...), condition=%wide.region_1.2_spmd.clone, body=%wide.region_0.1_spmd.clone.sunk | while | flops 655368 | bytes 1573061 | solution.py:72
  22.7 1.3 %dynamic_slice.41 = s32[1]{0:T(128)} dynamic-slice(s32[16]{0:T(128)} %get-tuple-element.227, s32[]{:T(128)S(6)} %copy.10), dynamic_slice_sizes={1} | dynamic-slice | bytes 12 | tf_op jit(solution)/shard_map/while/body/eval_jaxpr/dynamic_slice | solution.py:63
  24.6 1.2 %fusion.37 = f32[32,16,256]{2,1,0:T(8,128)S(1)} fusion(f32[32,16,256]{2,1,0:T(8,128)S(1)} %get-tuple-element.215, bf16[32,16,320]{2,1,0:T(8,128)(2,1)S(1)} %get-tuple-element.228, s32[]{:T(128)S(6)} %select_n.22, bf16[16,32,16,256]{3,2,1,0:T(8,128)(2,1)} %get-tuple-element.226, s32[]{:T(128)S(6)} %copy.10, pred[]{:T(512)S(6)} %compare.23), kind=kLoop, calls=%fused_computation.1.clone.1 | loop fusion | flops 655360 | bytes 1572873 | tf_op jit(solution)/shard_map/while/body/eval_jaxpr/add | solution.py:69
  25.9 1.3 %dynamic_slice.41 = s32[1]{0:T(128)} dynamic-slice(s32[16]{0:T(128)} %get-tuple-element.227, s32[]{:T(128)S(6)} %copy.10), dynamic_slice_sizes={1} | dynamic-slice | bytes 12 | tf_op jit(solution)/shard_map/while/body/eval_jaxpr/dynamic_slice | solution.py:63
  27.8 1.2 %fusion.37 = f32[32,16,256]{2,1,0:T(8,128)S(1)} fusion(f32[32,16,256]{2,1,0:T(8,128)S(1)} %get-tuple-element.215, bf16[32,16,320]{2,1,0:T(8,128)(2,1)S(1)} %get-tuple-element.228, s32[]{:T(128)S(6)} %select_n.22, bf16[16,32,16,256]{3,2,1,0:T(8,128)(2,1)} %get-tuple-element.226, s32[]{:T(128)S(6)} %copy.10, pred[]{:T(512)S(6)} %compare.23), kind=kLoop, calls=%fused_computation.1.clone.1 | loop fusion | flops 655360 | bytes 1572873 | tf_op jit(solution)/shard_map/while/body/eval_jaxpr/add | solution.py:69
  29.0 1.3 %dynamic_slice.41 = s32[1]{0:T(128)} dynamic-slice(s32[16]{0:T(128)} %get-tuple-element.227, s32[]{:T(128)S(6)} %copy.10), dynamic_slice_sizes={1} | dynamic-slice | bytes 12 | tf_op jit(solution)/shard_map/while/body/eval_jaxpr/dynamic_slice | solution.py:63
  30.9 1.2 %fusion.37 = f32[32,16,256]{2,1,0:T(8,128)S(1)} fusion(f32[32,16,256]{2,1,0:T(8,128)S(1)} %get-tuple-element.215, bf16[32,16,320]{2,1,0:T(8,128)(2,1)S(1)} %get-tuple-element.228, s32[]{:T(128)S(6)} %select_n.22, bf16[16,32,16,256]{3,2,1,0:T(8,128)(2,1)} %get-tuple-element.226, s32[]{:T(128)S(6)} %copy.10, pred[]{:T(512)S(6)} %compare.23), kind=kLoop, calls=%fused_computation.1.clone.1 | loop fusion | flops 655360 | bytes 1572873 | tf_op jit(solution)/shard_map/while/body/eval_jaxpr/add | solution.py:69
  32.1 1.3 %dynamic_slice.41 = s32[1]{0:T(128)} dynamic-slice(s32[16]{0:T(128)} %get-tuple-element.227, s32[]{:T(128)S(6)} %copy.10), dynamic_slice_sizes={1} | dynamic-slice | bytes 12 | tf_op jit(solution)/shard_map/while/body/eval_jaxpr/dynamic_slice | solution.py:63
  34.0 1.2 %fusion.37 = f32[32,16,256]{2,1,0:T(8,128)S(1)} fusion(f32[32,16,256]{2,1,0:T(8,128)S(1)} %get-tuple-element.215, bf16[32,16,320]{2,1,0:T(8,128)(2,1)S(1)} %get-tuple-element.228, s32[]{:T(128)S(6)} %select_n.22, bf16[16,32,16,256]{3,2,1,0:T(8,128)(2,1)} %get-tuple-element.226, s32[]{:T(128)S(6)} %copy.10, pred[]{:T(512)S(6)} %compare.23), kind=kLoop, calls=%fused_computation.1.clone.1 | loop fusion | flops 655360 | bytes 1572873 | tf_op jit(solution)/shard_map/while/body/eval_jaxpr/add | solution.py:69
  35.2 1.3 %dynamic_slice.41 = s32[1]{0:T(128)} dynamic-slice(s32[16]{0:T(128)} %get-tuple-element.227, s32[]{:T(128)S(6)} %copy.10), dynamic_slice_sizes={1} | dynamic-slice | bytes 12 | tf_op jit(solution)/shard_map/while/body/eval_jaxpr/dynamic_slice | solution.py:63
  37.1 1.2 %fusion.37 = f32[32,16,256]{2,1,0:T(8,128)S(1)} fusion(f32[32,16,256]{2,1,0:T(8,128)S(1)} %get-tuple-element.215, bf16[32,16,320]{2,1,0:T(8,128)(2,1)S(1)} %get-tuple-element.228, s32[]{:T(128)S(6)} %select_n.22, bf16[16,32,16,256]{3,2,1,0:T(8,128)(2,1)} %get-tuple-element.226, s32[]{:T(128)S(6)} %copy.10, pred[]{:T(512)S(6)} %compare.23), kind=kLoop, calls=%fused_computation.1.clone.1 | loop fusion | flops 655360 | bytes 1572873 | tf_op jit(solution)/shard_map/while/body/eval_jaxpr/add | solution.py:69
  38.3 1.3 %dynamic_slice.41 = s32[1]{0:T(128)} dynamic-slice(s32[16]{0:T(128)} %get-tuple-element.227, s32[]{:T(128)S(6)} %copy.10), dynamic_slice_sizes={1} | dynamic-slice | bytes 12 | tf_op jit(solution)/shard_map/while/body/eval_jaxpr/dynamic_slice | solution.py:63
  40.2 1.2 %fusion.37 = f32[32,16,256]{2,1,0:T(8,128)S(1)} fusion(f32[32,16,256]{2,1,0:T(8,128)S(1)} %get-tuple-element.215, bf16[32,16,320]{2,1,0:T(8,128)(2,1)S(1)} %get-tuple-element.228, s32[]{:T(128)S(6)} %select_n.22, bf16[16,32,16,256]{3,2,1,0:T(8,128)(2,1)} %get-tuple-element.226, s32[]{:T(128)S(6)} %copy.10, pred[]{:T(512)S(6)} %compare.23), kind=kLoop, calls=%fused_computation.1.clone.1 | loop fusion | flops 655360 | bytes 1572873 | tf_op jit(solution)/shard_map/while/body/eval_jaxpr/add | solution.py:69
  41.4 1.3 %dynamic_slice.41 = s32[1]{0:T(128)} dynamic-slice(s32[16]{0:T(128)} %get-tuple-element.227, s32[]{:T(128)S(6)} %copy.10), dynamic_slice_sizes={1} | dynamic-slice | bytes 12 | tf_op jit(solution)/shard_map/while/body/eval_jaxpr/dynamic_slice | solution.py:63
  44.6 1.3 %dynamic_slice.41 = s32[1]{0:T(128)} dynamic-slice(s32[16]{0:T(128)} %get-tuple-element.227, s32[]{:T(128)S(6)} %copy.10), dynamic_slice_sizes={1} | dynamic-slice | bytes 12 | tf_op jit(solution)/shard_map/while/body/eval_jaxpr/dynamic_slice | solution.py:63
  47.7 1.3 %dynamic_slice.41 = s32[1]{0:T(128)} dynamic-slice(s32[16]{0:T(128)} %get-tuple-element.227, s32[]{:T(128)S(6)} %copy.10), dynamic_slice_sizes={1} | dynamic-slice | bytes 12 | tf_op jit(solution)/shard_map/while/body/eval_jaxpr/dynamic_slice | solution.py:63
  50.8 1.3 %dynamic_slice.41 = s32[1]{0:T(128)} dynamic-slice(s32[16]{0:T(128)} %get-tuple-element.227, s32[]{:T(128)S(6)} %copy.10), dynamic_slice_sizes={1} | dynamic-slice | bytes 12 | tf_op jit(solution)/shard_map/while/body/eval_jaxpr/dynamic_slice | solution.py:63
  53.9 1.3 %dynamic_slice.41 = s32[1]{0:T(128)} dynamic-slice(s32[16]{0:T(128)} %get-tuple-element.227, s32[]{:T(128)S(6)} %copy.10), dynamic_slice_sizes={1} | dynamic-slice | bytes 12 | tf_op jit(solution)/shard_map/while/body/eval_jaxpr/dynamic_slice | solution.py:63
  57.0 1.3 %dynamic_slice.41 = s32[1]{0:T(128)} dynamic-slice(s32[16]{0:T(128)} %get-tuple-element.227, s32[]{:T(128)S(6)} %copy.10), dynamic_slice_sizes={1} | dynamic-slice | bytes 12 | tf_op jit(solution)/shard_map/while/body/eval_jaxpr/dynamic_slice | solution.py:63
  60.2 1.3 %dynamic_slice.41 = s32[1]{0:T(128)} dynamic-slice(s32[16]{0:T(128)} %get-tuple-element.227, s32[]{:T(128)S(6)} %copy.10), dynamic_slice_sizes={1} | dynamic-slice | bytes 12 | tf_op jit(solution)/shard_map/while/body/eval_jaxpr/dynamic_slice | solution.py:63
  63.3 1.3 %dynamic_slice.41 = s32[1]{0:T(128)} dynamic-slice(s32[16]{0:T(128)} %get-tuple-element.227, s32[]{:T(128)S(6)} %copy.10), dynamic_slice_sizes={1} | dynamic-slice | bytes 12 | tf_op jit(solution)/shard_map/while/body/eval_jaxpr/dynamic_slice | solution.py:63
  66.4 1.3 %dynamic_slice.41 = s32[1]{0:T(128)} dynamic-slice(s32[16]{0:T(128)} %get-tuple-element.227, s32[]{:T(128)S(6)} %copy.10), dynamic_slice_sizes={1} | dynamic-slice | bytes 12 | tf_op jit(solution)/shard_map/while/body/eval_jaxpr/dynamic_slice | solution.py:63
  69.5 1.3 %dynamic_slice.41 = s32[1]{0:T(128)} dynamic-slice(s32[16]{0:T(128)} %get-tuple-element.227, s32[]{:T(128)S(6)} %copy.10), dynamic_slice_sizes={1} | dynamic-slice | bytes 12 | tf_op jit(solution)/shard_map/while/body/eval_jaxpr/dynamic_slice | solution.py:63
  73.5 1.3 %collective-permute-start = (f32[4,16,256]{2,1,0:T(8,128)S(1)}, f32[4,16,256]{2,1,0:T(8,128)S(1)}, u32[]{:S(2)}, u32[]{:S(2)}) collective-permute-start(f32[4,16,256]{2,1,0:T(8,128)S(1)} %get-tuple-element.171), channel_id=1, source_target_pairs={{4,0},{8,4},{12,8},{5,1},{9,5},{13,9},{6,2},{10,6},{14,10},{7,3},{... | collective-permute-start | bytes 196616 | tf_op jit(solution)/shard_map/ppermute | solution.py:20
  74.8 4.5 %collective-permute-start.1 = (f32[4,16,256]{2,1,0:T(8,128)S(1)}, f32[4,16,256]{2,1,0:T(8,128)S(1)}, u32[]{:S(2)}, u32[]{:S(2)}) collective-permute-start(f32[4,16,256]{2,1,0:T(8,128)S(1)} %get-tuple-element.172), channel_id=1, source_target_pairs={{0,4},{4,8},{8,12},{1,5},{5,9},{9,13},{2,6},{6,10},{10,14},{3,7},{... | collective-permute-start | bytes 196616 | tf_op jit(solution)/shard_map/ppermute | solution.py:18
  79.6 1.6 %collective-permute-done.1 = f32[4,16,256]{2,1,0:T(8,128)S(1)} collective-permute-done((f32[4,16,256]{2,1,0:T(8,128)S(1)}, f32[4,16,256]{2,1,0:T(8,128)S(1)}, u32[]{:S(2)}, u32[]{:S(2)}) %collective-permute-start.1) | collective-permute-done | bytes 65568 | tf_op jit(solution)/shard_map/ppermute | solution.py:18
  81.3 3.4 %collective-permute-start.3 = (f32[16,4,256]{2,1,0:T(4,128)S(1)}, f32[16,4,256]{2,1,0:T(4,128)S(1)}, u32[]{:S(2)}, u32[]{:S(2)}) collective-permute-start(f32[16,4,256]{2,1,0:T(4,128)S(1)} %get-tuple-element.169), channel_id=1, source_target_pairs={{0,2},{1,3},{4,6},{5,7},{8,10},{9,11},{12,14},{13,15},{16,18},{17,... | collective-permute-start | bytes 196616 | tf_op jit(solution)/shard_map/ppermute | solution.py:18
  84.7 1.3 %collective-permute-start.2 = (f32[16,4,256]{2,1,0:T(4,128)S(1)}, f32[16,4,256]{2,1,0:T(4,128)S(1)}, u32[]{:S(2)}, u32[]{:S(2)}) collective-permute-start(f32[16,4,256]{2,1,0:T(4,128)S(1)} %get-tuple-element.170), channel_id=1, source_target_pairs={{2,0},{3,1},{6,4},{7,5},{10,8},{11,9},{14,12},{15,13},{18,16},{19,... | collective-permute-start | bytes 196616 | tf_op jit(solution)/shard_map/ppermute | solution.py:20
  86.5 4.3 %collective-permute-done.2 = f32[16,4,256]{2,1,0:T(4,128)S(1)} collective-permute-done((f32[16,4,256]{2,1,0:T(4,128)S(1)}, f32[16,4,256]{2,1,0:T(4,128)S(1)}, u32[]{:S(2)}, u32[]{:S(2)}) %collective-permute-start.2) | collective-permute-done | bytes 65568 | tf_op jit(solution)/shard_map/ppermute | solution.py:20
  91.2 5.8 %reduce-scatter.2.cloned.1.call-done = f32[8,16,256]{2,1,0:T(8,128)} async-done(((f32[32,16,256]{2,1,0:T(8,128)}), f32[8,16,256]{2,1,0:T(8,128)}) %reduce-scatter.2.cloned.1.call-update) | async-done | bytes 131088 | tf_op jit(solution)/shard_map/reduce_scatter | solution.py:71
  97.0 1.9 %fusion.14 = f32[1,8,16,256]{3,2,1,0:T(8,128)} fusion(f32[8,16,256]{2,1,0:T(8,128)S(1)} %copy-done.2, f32[8,16,256]{2,1,0:T(8,128)} %reduce-scatter.2.cloned.1.call-done, f32[8,16,256]{2,1,0:T(8,128)S(1)} %bitcast.27, f32[4,16,256]{2,1,0:T(8,128)S(1)} %collective-permute-done.1, f32[4,16,256]{2,1,0:T(8,128)S(1)} %collective-permute-done, ...), kind=kLoop, calls=%fused_computation.35 | loop fusion | flops 1376256 | bytes 2883584 | tf_op jit(solution)/shard_map/broadcast_in_dim | solution.py:85
  (28 shorter events, 14.2 us)
Async XLA Ops:
  6.5 90.5 %reduce-scatter.2.cloned.1.call-start = ((), (), s32[]{:S(2)}) async-start(), calls=%async_computation.1 | async-start | bytes 655360 | tf_op jit(solution)/shard_map/reduce_scatter | solution.py:71
  22.6 50.8 %copy-start.1 = (f32[1,8,16,256]{3,2,1,0:T(8,128)S(1)}, f32[1,8,16,256]{3,2,1,0:T(8,128)}, u32[]{:S(2)}) copy-start(f32[1,8,16,256]{3,2,1,0:T(8,128)} %param.11) | copy-start | bytes 393220
  22.6 74.4 %copy-start.2 = (f32[8,16,256]{2,1,0:T(8,128)S(1)}, f32[8,16,256]{2,1,0:T(8,128)}, u32[]{:S(2)}) copy-start(f32[8,16,256]{2,1,0:T(8,128)} %param.13) | copy-start | bytes 393220
  22.6 74.4 %copy-start.3 = (f32[1,8,16,256]{3,2,1,0:T(8,128)S(1)}, f32[1,8,16,256]{3,2,1,0:T(8,128)}, u32[]{:S(2)}) copy-start(f32[1,8,16,256]{3,2,1,0:T(8,128)} %param.12) | copy-start | bytes 393220
  72.6 0.8 copy-start
  73.5 6.2 %collective-permute-start = (f32[4,16,256]{2,1,0:T(8,128)S(1)}, f32[4,16,256]{2,1,0:T(8,128)S(1)}, u32[]{:S(2)}, u32[]{:S(2)}) collective-permute-start(f32[4,16,256]{2,1,0:T(8,128)S(1)} %get-tuple-element.171), channel_id=1, source_target_pairs={{4,0},{8,4},{12,8},{5,1},{9,5},{13,9},{6,2},{10,6},{14,10},{7,3},{... | collective-permute-start | bytes 196616 | tf_op jit(solution)/shard_map/ppermute | solution.py:20
  74.8 6.5 %collective-permute-start.1 = (f32[4,16,256]{2,1,0:T(8,128)S(1)}, f32[4,16,256]{2,1,0:T(8,128)S(1)}, u32[]{:S(2)}, u32[]{:S(2)}) collective-permute-start(f32[4,16,256]{2,1,0:T(8,128)S(1)} %get-tuple-element.172), channel_id=1, source_target_pairs={{0,4},{4,8},{8,12},{1,5},{5,9},{9,13},{2,6},{6,10},{10,14},{3,7},{... | collective-permute-start | bytes 196616 | tf_op jit(solution)/shard_map/ppermute | solution.py:18
  81.3 5.3 %collective-permute-start.3 = (f32[16,4,256]{2,1,0:T(4,128)S(1)}, f32[16,4,256]{2,1,0:T(4,128)S(1)}, u32[]{:S(2)}, u32[]{:S(2)}) collective-permute-start(f32[16,4,256]{2,1,0:T(4,128)S(1)} %get-tuple-element.169), channel_id=1, source_target_pairs={{0,2},{1,3},{4,6},{5,7},{8,10},{9,11},{12,14},{13,15},{16,18},{17,... | collective-permute-start | bytes 196616 | tf_op jit(solution)/shard_map/ppermute | solution.py:18
  84.7 6.2 %collective-permute-start.2 = (f32[16,4,256]{2,1,0:T(4,128)S(1)}, f32[16,4,256]{2,1,0:T(4,128)S(1)}, u32[]{:S(2)}, u32[]{:S(2)}) collective-permute-start(f32[16,4,256]{2,1,0:T(4,128)S(1)} %get-tuple-element.170), channel_id=1, source_target_pairs={{2,0},{3,1},{6,4},{7,5},{10,8},{11,9},{14,12},{15,13},{18,16},{19,... | collective-permute-start | bytes 196616 | tf_op jit(solution)/shard_map/ppermute | solution.py:20
Sparse Core Ops, SparseCore 0:
  73.6 23.3 reduce-scatter.1
where the time goes:
time: 107 us; the launch traced here: 106 us
  other arithmetic  21.3 us (20%)
  local copies, waits for them, and re-layouts  21.3 us (20%)
  blocking collectives  15.9 us (15%)
  between operations  13.5 us (13%)
  waiting for transfers between devices  12.6 us (12%)
  loops' own time  10.6 us (10%)
  starting transfers between devices  10.5 us (10%)
    dynamic_slice x16, local copies, waits for them, and re-layouts, add_column(): offset_cells = offset_of[column] - half_span  20.3 us
    add x16, other arithmetic, add_column(): return running + whole_col.astype(jnp.float32) * shifted.astype(jnp.float32)  19 us
    all_gather x1, blocking collectives, on_device(): gathered = lax.all_gather(background, 'off', axis=1, tiled=True)  15.9 us
    another operation x1, loops' own time, on_device(): lax.fori_loop(0, local_cols, add_column, jnp.zeros((slab_rows * lax.axis_...  10.6 us
    ppermute x2, starting transfers between devices, extended_2(): lax.ppermute(tail, axis, [(i, (i + 1) % count) for i in range(ends)])  7.91 us
    reduce_scatter x1, waiting for transfers between devices, on_device(): lax.psum_scatter(lax.fori_loop(0, local_cols, add_column, jnp.zeros((slab...  5.78 us
    ppermute x2, waiting for transfers between devices, extended_2(): lax.ppermute(head, axis, [((i + 1) % count, i) for i in range(ends)])  4.58 us
    ppermute x2, starting transfers between devices, extended_2(): lax.ppermute(head, axis, [((i + 1) % count, i) for i in range(ends)])  2.58 us
  transfers between devices with their start and end apart: 5, of which 5 were waited for; matrix products, arithmetic and copies ran while one was open for 0% of the time, Pallas kernels for 0%

commit v1 on v0

--- a/solution.py
+++ b/solution.py
@@ -5,6 +5,17 @@
 
 H = 64
 STENCIL = (-205.0 / 72.0, 8.0 / 5.0, -1.0 / 5.0, 8.0 / 315.0, -1.0 / 560.0)
+
+
+def pass_along(x, axis, d):
+    size = lax.axis_size(axis)
+    route = [(i, (i + 1) % size) for i in range(size)]
+    parts = [x]
+    for far in range(1, size):
+        parts = [lax.ppermute(parts[0], axis, route), *parts]
+    whole = jnp.concatenate(parts, axis=d)
+    places = (lax.axis_index(axis) + 1) * parts[-1].shape[d]
+    return jnp.roll(whole, places, axis=d)
 
 
 def extended_2(cells, sides, width):
@@ -55,7 +66,7 @@
     width_x = wave_now.shape[3]
     local_cols = image.shape[0]
     half_span = H // 2
-    gathered = lax.all_gather(background, "off", axis=1, tiled=True)
+    gathered = pass_along(background, "off", 1)
     extended_bg = jnp.pad(gathered[0], ((0, 0), (0, 0), (half_span, half_span)))
     first_index = jnp.asarray(jnp.int32(0), jnp.int32)
 

time: 107 us -> 110 us (1.028)
  blocking collectives: 15.9 us -> 0 us
  waiting for transfers between devices: 12.6 us -> 24.8 us
  starting transfers between devices: 10.5 us -> 14.7 us
  local copies, waits for them, and re-layouts: 21.3 us -> 23.7 us
    ppermute x0 -> x3, waiting for transfers between devices: none -> 16.6 us  [pass_along(): parts = [lax.ppermute(parts[0], axis, route), *parts]]
    all_gather x1 -> x0, blocking collectives: 15.9 us -> none  [on_device(): gathered = lax.all_gather(background, 'off', axis=1, tiled=True)]
    ppermute x2, waiting for transfers between devices: 4.58 us -> 0.61 us  [extended_2(): lax.ppermute(head, axis, [((i + 1) % count, i) for i in range(ends)])]
    ppermute x0 -> x3, starting transfers between devices: none -> 3.06 us  [pass_along(): parts = [lax.ppermute(parts[0], axis, route), *parts]]
    reduce_scatter x1, waiting for transfers between devices: 5.78 us -> 4.34 us  [on_device(): lax.psum_scatter(lax.fori_loop(0, local_cols, add_column, jnp.zeros((slab...]
    ppermute x2, starting transfers between devices: 7.91 us -> 9.1 us  [extended_2(): lax.ppermute(tail, axis, [(i, (i + 1) % count) for i in range(ends)])]
  transfers between devices with their start and end apart: 5 -> 8, of which waited for: 5 -> 8; matrix products, arithmetic and copies ran while one was open for 0% -> 0% of each run, Pallas kernels for 0% -> 0%
where the time goes in v1:
time: 110 us; the launch traced here: 109 us
  waiting for transfers between devices  24.8 us (23%)
  local copies, waits for them, and re-layouts  23.7 us (22%)
  other arithmetic  21.3 us (19%)
  starting transfers between devices  14.7 us (13%)
  between operations  13.5 us (12%)
  loops' own time  10.4 us (9%)
    dynamic_slice x16, local copies, waits for them, and re-layouts, add_column(): offset_cells = offset_of[column] - half_span  20.9 us
    add x16, other arithmetic, add_column(): return running + whole_col.astype(jnp.float32) * shifted.astype(jnp.float32)  19 us
    ppermute x3, waiting for transfers between devices, pass_along(): parts = [lax.ppermute(parts[0], axis, route), *parts]  16.6 us
    another operation x1, loops' own time, on_device(): lax.fori_loop(0, local_cols, add_column, jnp.zeros((slab_rows * lax.axis_...  10.4 us
    ppermute x2, starting transfers between devices, extended_2(): lax.ppermute(tail, axis, [(i, (i + 1) % count) for i in range(ends)])  9.1 us
    reduce_scatter x1, waiting for transfers between devices, on_device(): lax.psum_scatter(lax.fori_loop(0, local_cols, add_column, jnp.zeros((slab...  4.34 us
    ppermute x2, waiting for transfers between devices, extended_2(): lax.ppermute(tail, axis, [(i, (i + 1) % count) for i in range(ends)])  3.28 us
    ppermute x3, starting transfers between devices, pass_along(): parts = [lax.ppermute(parts[0], axis, route), *parts]  3.06 us
  transfers between devices with their start and end apart: 8, of which 8 were waited for; matrix products, arithmetic and copies ran while one was open for 0% of the time, Pallas kernels for 0%

profile of v1, /device:TPU:0, one launch (start us, length us, event | category | flops | bytes accessed | tf_op | source)
XLA Modules:
  0.0 108.5 jit_solution(14719529503544608043)
XLA Ops:
  6.5 3.1 %collective-permute-start.4 = (bf16[1,8,16,256]{3,2,1,0:T(8,128)(2,1)}, bf16[1,8,16,256]{3,2,1,0:T(8,128)(2,1)S(1)}, u32[]{:S(2)}, u32[]{:S(2)}) collective-permute-start(bf16[1,8,16,256]{3,2,1,0:T(8,128)(2,1)} %param.10), channel_id=1, source_target_pairs={{0,4},{4,8},{8,12},{12,0},{1,5},{5,9},{9,13},{13,1},{2,6},{6,10},{... | collective-permute-start | bytes 196616 | tf_op jit(solution)/shard_map/ppermute | solution.py:15
  9.6 4.5 %collective-permute-done.4 = bf16[1,8,16,256]{3,2,1,0:T(8,128)(2,1)S(1)} collective-permute-done((bf16[1,8,16,256]{3,2,1,0:T(8,128)(2,1)}, bf16[1,8,16,256]{3,2,1,0:T(8,128)(2,1)S(1)}, u32[]{:S(2)}, u32[]{:S(2)}) %collective-permute-start.4) | collective-permute-done | bytes 65568 | tf_op jit(solution)/shard_map/ppermute | solution.py:15
  14.1 6.1 %collective-permute-done.5 = bf16[1,8,16,256]{3,2,1,0:T(8,128)(2,1)S(1)} collective-permute-done((bf16[1,8,16,256]{3,2,1,0:T(8,128)(2,1)S(1)}, bf16[1,8,16,256]{3,2,1,0:T(8,128)(2,1)S(1)}, u32[]{:S(2)}, u32[]{:S(2)}) %collective-permute-start.5) | collective-permute-done | bytes 65568 | tf_op jit(solution)/shard_map/ppermute | solution.py:15
  20.1 6.1 %collective-permute-done.6 = bf16[1,8,16,256]{3,2,1,0:T(8,128)(2,1)S(1)} collective-permute-done((bf16[1,8,16,256]{3,2,1,0:T(8,128)(2,1)S(1)}, bf16[1,8,16,256]{3,2,1,0:T(8,128)(2,1)S(1)}, u32[]{:S(2)}, u32[]{:S(2)}) %collective-permute-start.6) | collective-permute-done | bytes 65568 | tf_op jit(solution)/shard_map/ppermute | solution.py:15
  28.2 50.4 %while.16 = (s32[]{:T(128)}, f32[32,16,256]{2,1,0:T(8,128)S(1)}, bf16[16,32,16,256]{3,2,1,0:T(8,128)(2,1)}, s32[16]{0:T(128)}, bf16[32,16,320]{2,1,0:T(8,128)(2,...) while((s32[]{:T(128)}, f32[32,16,256]{2,1,0:T(8,128)S(1)}, ...), condition=%wide.region_1.2_spmd.clone, body=%wide.region_0.1_spmd.clone.sunk | while | flops 655368 | bytes 1573053 | solution.py:83
  28.2 1.4 %dynamic_slice.47 = s32[1]{0:T(128)} dynamic-slice(s32[16]{0:T(128)} %get-tuple-element.227, s32[]{:T(128)} %get-tuple-element.214), dynamic_slice_sizes={1} | dynamic-slice | bytes 12 | tf_op jit(solution)/shard_map/while/body/eval_jaxpr/dynamic_slice | solution.py:74
  30.3 1.2 %fusion.37 = f32[32,16,256]{2,1,0:T(8,128)S(1)} fusion(f32[32,16,256]{2,1,0:T(8,128)S(1)} %get-tuple-element.215, bf16[32,16,320]{2,1,0:T(8,128)(2,1)S(1)} %get-tuple-element.228, s32[]{:T(128)S(6)} %select_n.37, bf16[16,32,16,256]{3,2,1,0:T(8,128)(2,1)} %get-tuple-element.226, s32[]{:T(128)} %get-tuple-element.214, pred[]{:T(512)S(6)} %compare.24), kind=kLoop, calls=%fused_computation.1.clone.1 | loop fusion | flops 655360 | bytes 1572873 | tf_op jit(solution)/shard_map/while/body/eval_jaxpr/add | solution.py:80
  31.5 1.3 %dynamic_slice.47 = s32[1]{0:T(128)} dynamic-slice(s32[16]{0:T(128)} %get-tuple-element.227, s32[]{:T(128)} %get-tuple-element.214), dynamic_slice_sizes={1} | dynamic-slice | bytes 12 | tf_op jit(solution)/shard_map/while/body/eval_jaxpr/dynamic_slice | solution.py:74
  34.6 1.3 %dynamic_slice.47 = s32[1]{0:T(128)} dynamic-slice(s32[16]{0:T(128)} %get-tuple-element.227, s32[]{:T(128)} %get-tuple-element.214), dynamic_slice_sizes={1} | dynamic-slice | bytes 12 | tf_op jit(solution)/shard_map/while/body/eval_jaxpr/dynamic_slice | solution.py:74
  37.7 1.3 %dynamic_slice.47 = s32[1]{0:T(128)} dynamic-slice(s32[16]{0:T(128)} %get-tuple-element.227, s32[]{:T(128)} %get-tuple-element.214), dynamic_slice_sizes={1} | dynamic-slice | bytes 12 | tf_op jit(solution)/shard_map/while/body/eval_jaxpr/dynamic_slice | solution.py:74
  40.9 1.3 %dynamic_slice.47 = s32[1]{0:T(128)} dynamic-slice(s32[16]{0:T(128)} %get-tuple-element.227, s32[]{:T(128)} %get-tuple-element.214), dynamic_slice_sizes={1} | dynamic-slice | bytes 12 | tf_op jit(solution)/shard_map/while/body/eval_jaxpr/dynamic_slice | solution.py:74
  44.0 1.3 %dynamic_slice.47 = s32[1]{0:T(128)} dynamic-slice(s32[16]{0:T(128)} %get-tuple-element.227, s32[]{:T(128)} %get-tuple-element.214), dynamic_slice_sizes={1} | dynamic-slice | bytes 12 | tf_op jit(solution)/shard_map/while/body/eval_jaxpr/dynamic_slice | solution.py:74
  47.2 1.3 %dynamic_slice.47 = s32[1]{0:T(128)} dynamic-slice(s32[16]{0:T(128)} %get-tuple-element.227, s32[]{:T(128)} %get-tuple-element.214), dynamic_slice_sizes={1} | dynamic-slice | bytes 12 | tf_op jit(solution)/shard_map/while/body/eval_jaxpr/dynamic_slice | solution.py:74
  49.1 1.2 %fusion.37 = f32[32,16,256]{2,1,0:T(8,128)S(1)} fusion(f32[32,16,256]{2,1,0:T(8,128)S(1)} %get-tuple-element.215, bf16[32,16,320]{2,1,0:T(8,128)(2,1)S(1)} %get-tuple-element.228, s32[]{:T(128)S(6)} %select_n.37, bf16[16,32,16,256]{3,2,1,0:T(8,128)(2,1)} %get-tuple-element.226, s32[]{:T(128)} %get-tuple-element.214, pred[]{:T(512)S(6)} %compare.24), kind=kLoop, calls=%fused_computation.1.clone.1 | loop fusion | flops 655360 | bytes 1572873 | tf_op jit(solution)/shard_map/while/body/eval_jaxpr/add | solution.py:80
  50.3 1.3 %dynamic_slice.47 = s32[1]{0:T(128)} dynamic-slice(s32[16]{0:T(128)} %get-tuple-element.227, s32[]{:T(128)} %get-tuple-element.214), dynamic_slice_sizes={1} | dynamic-slice | bytes 12 | tf_op jit(solution)/shard_map/while/body/eval_jaxpr/dynamic_slice | solution.py:74
  52.3 1.2 %fusion.37 = f32[32,16,256]{2,1,0:T(8,128)S(1)} fusion(f32[32,16,256]{2,1,0:T(8,128)S(1)} %get-tuple-element.215, bf16[32,16,320]{2,1,0:T(8,128)(2,1)S(1)} %get-tuple-element.228, s32[]{:T(128)S(6)} %select_n.37, bf16[16,32,16,256]{3,2,1,0:T(8,128)(2,1)} %get-tuple-element.226, s32[]{:T(128)} %get-tuple-element.214, pred[]{:T(512)S(6)} %compare.24), kind=kLoop, calls=%fused_computation.1.clone.1 | loop fusion | flops 655360 | bytes 1572873 | tf_op jit(solution)/shard_map/while/body/eval_jaxpr/add | solution.py:80
  53.5 1.3 %dynamic_slice.47 = s32[1]{0:T(128)} dynamic-slice(s32[16]{0:T(128)} %get-tuple-element.227, s32[]{:T(128)} %get-tuple-element.214), dynamic_slice_sizes={1} | dynamic-slice | bytes 12 | tf_op jit(solution)/shard_map/while/body/eval_jaxpr/dynamic_slice | solution.py:74
  56.6 1.3 %dynamic_slice.47 = s32[1]{0:T(128)} dynamic-slice(s32[16]{0:T(128)} %get-tuple-element.227, s32[]{:T(128)} %get-tuple-element.214), dynamic_slice_sizes={1} | dynamic-slice | bytes 12 | tf_op jit(solution)/shard_map/while/body/eval_jaxpr/dynamic_slice | solution.py:74
  59.7 1.3 %dynamic_slice.47 = s32[1]{0:T(128)} dynamic-slice(s32[16]{0:T(128)} %get-tuple-element.227, s32[]{:T(128)} %get-tuple-element.214), dynamic_slice_sizes={1} | dynamic-slice | bytes 12 | tf_op jit(solution)/shard_map/while/body/eval_jaxpr/dynamic_slice | solution.py:74
  62.9 1.3 %dynamic_slice.47 = s32[1]{0:T(128)} dynamic-slice(s32[16]{0:T(128)} %get-tuple-element.227, s32[]{:T(128)} %get-tuple-element.214), dynamic_slice_sizes={1} | dynamic-slice | bytes 12 | tf_op jit(solution)/shard_map/while/body/eval_jaxpr/dynamic_slice | solution.py:74
  66.0 1.3 %dynamic_slice.47 = s32[1]{0:T(128)} dynamic-slice(s32[16]{0:T(128)} %get-tuple-element.227, s32[]{:T(128)} %get-tuple-element.214), dynamic_slice_sizes={1} | dynamic-slice | bytes 12 | tf_op jit(solution)/shard_map/while/body/eval_jaxpr/dynamic_slice | solution.py:74
  69.2 1.3 %dynamic_slice.47 = s32[1]{0:T(128)} dynamic-slice(s32[16]{0:T(128)} %get-tuple-element.227, s32[]{:T(128)} %get-tuple-element.214), dynamic_slice_sizes={1} | dynamic-slice | bytes 12 | tf_op jit(solution)/shard_map/while/body/eval_jaxpr/dynamic_slice | solution.py:74
  72.3 1.3 %dynamic_slice.47 = s32[1]{0:T(128)} dynamic-slice(s32[16]{0:T(128)} %get-tuple-element.227, s32[]{:T(128)} %get-tuple-element.214), dynamic_slice_sizes={1} | dynamic-slice | bytes 12 | tf_op jit(solution)/shard_map/while/body/eval_jaxpr/dynamic_slice | solution.py:74
  75.5 1.3 %dynamic_slice.47 = s32[1]{0:T(128)} dynamic-slice(s32[16]{0:T(128)} %get-tuple-element.227, s32[]{:T(128)} %get-tuple-element.214), dynamic_slice_sizes={1} | dynamic-slice | bytes 12 | tf_op jit(solution)/shard_map/while/body/eval_jaxpr/dynamic_slice | solution.py:74
  79.4 1.3 %collective-permute-start = (f32[4,16,256]{2,1,0:T(8,128)S(1)}, f32[4,16,256]{2,1,0:T(8,128)S(1)}, u32[]{:S(2)}, u32[]{:S(2)}) collective-permute-start(f32[4,16,256]{2,1,0:T(8,128)S(1)} %get-tuple-element.171), channel_id=1, source_target_pairs={{4,0},{8,4},{12,8},{5,1},{9,5},{13,9},{6,2},{10,6},{14,10},{7,3},{... | collective-permute-start | bytes 196616 | tf_op jit(solution)/shard_map/ppermute | solution.py:31
  80.7 4.5 %collective-permute-start.1 = (f32[4,16,256]{2,1,0:T(8,128)S(1)}, f32[4,16,256]{2,1,0:T(8,128)S(1)}, u32[]{:S(2)}, u32[]{:S(2)}) collective-permute-start(f32[4,16,256]{2,1,0:T(8,128)S(1)} %get-tuple-element.172), channel_id=1, source_target_pairs={{0,4},{4,8},{8,12},{1,5},{5,9},{9,13},{2,6},{6,10},{10,14},{3,7},{... | collective-permute-start | bytes 196616 | tf_op jit(solution)/shard_map/ppermute | solution.py:29
  85.6 1.7 %collective-permute-done.1 = f32[4,16,256]{2,1,0:T(8,128)S(1)} collective-permute-done((f32[4,16,256]{2,1,0:T(8,128)S(1)}, f32[4,16,256]{2,1,0:T(8,128)S(1)}, u32[]{:S(2)}, u32[]{:S(2)}) %collective-permute-start.1) | collective-permute-done | bytes 65568 | tf_op jit(solution)/shard_map/ppermute | solution.py:29
  87.3 1.3 %collective-permute-start.2 = (f32[16,4,256]{2,1,0:T(4,128)S(1)}, f32[16,4,256]{2,1,0:T(4,128)S(1)}, u32[]{:S(2)}, u32[]{:S(2)}) collective-permute-start(f32[16,4,256]{2,1,0:T(4,128)S(1)} %get-tuple-element.170), channel_id=1, source_target_pairs={{2,0},{3,1},{6,4},{7,5},{10,8},{11,9},{14,12},{15,13},{18,16},{19,... | collective-permute-start | bytes 196616 | tf_op jit(solution)/shard_map/ppermute | solution.py:31
  88.6 4.5 %collective-permute-start.3 = (f32[16,4,256]{2,1,0:T(4,128)S(1)}, f32[16,4,256]{2,1,0:T(4,128)S(1)}, u32[]{:S(2)}, u32[]{:S(2)}) collective-permute-start(f32[16,4,256]{2,1,0:T(4,128)S(1)} %get-tuple-element.169), channel_id=1, source_target_pairs={{0,2},{1,3},{4,6},{5,7},{8,10},{9,11},{12,14},{13,15},{16,18},{17,... | collective-permute-start | bytes 196616 | tf_op jit(solution)/shard_map/ppermute | solution.py:29
  93.5 1.6 %collective-permute-done.3 = f32[16,4,256]{2,1,0:T(4,128)S(1)} collective-permute-done((f32[16,4,256]{2,1,0:T(4,128)S(1)}, f32[16,4,256]{2,1,0:T(4,128)S(1)}, u32[]{:S(2)}, u32[]{:S(2)}) %collective-permute-start.3) | collective-permute-done | bytes 65568 | tf_op jit(solution)/shard_map/ppermute | solution.py:29
  95.5 4.3 %reduce-scatter.2.cloned.1.call-done = f32[8,16,256]{2,1,0:T(8,128)} async-done(((f32[32,16,256]{2,1,0:T(8,128)}), f32[8,16,256]{2,1,0:T(8,128)}) %reduce-scatter.2.cloned.1.call-update) | async-done | bytes 131088 | tf_op jit(solution)/shard_map/reduce_scatter | solution.py:82
  99.8 1.9 %fusion.14 = f32[1,8,16,256]{3,2,1,0:T(8,128)} fusion(f32[8,16,256]{2,1,0:T(8,128)S(1)} %copy-done.2, f32[8,16,256]{2,1,0:T(8,128)} %reduce-scatter.2.cloned.1.call-done, f32[8,16,256]{2,1,0:T(8,128)S(1)} %bitcast.27, f32[4,16,256]{2,1,0:T(8,128)S(1)} %collective-permute-done.1, f32[4,16,256]{2,1,0:T(8,128)S(1)} %collective-permute-done, ...), kind=kLoop, calls=%fused_computation.36 | loop fusion | flops 1376256 | bytes 2883584 | tf_op jit(solution)/shard_map/broadcast_in_dim | solution.py:96
  (42 shorter events, 19.2 us)
Async XLA Ops:
  6.5 93.3 %reduce-scatter.2.cloned.1.call-start = ((), (), s32[]{:S(2)}) async-start(), calls=%async_computation.1 | async-start | bytes 655360 | tf_op jit(solution)/shard_map/reduce_scatter | solution.py:82
  6.5 7.5 %collective-permute-start.4 = (bf16[1,8,16,256]{3,2,1,0:T(8,128)(2,1)}, bf16[1,8,16,256]{3,2,1,0:T(8,128)(2,1)S(1)}, u32[]{:S(2)}, u32[]{:S(2)}) collective-permute-start(bf16[1,8,16,256]{3,2,1,0:T(8,128)(2,1)} %param.10), channel_id=1, source_target_pairs={{0,4},{4,8},{8,12},{12,0},{1,5},{5,9},{9,13},{13,1},{2,6},{6,10},{... | collective-permute-start | bytes 196616 | tf_op jit(solution)/shard_map/ppermute | solution.py:15
  14.1 6.1 %collective-permute-start.5 = (bf16[1,8,16,256]{3,2,1,0:T(8,128)(2,1)S(1)}, bf16[1,8,16,256]{3,2,1,0:T(8,128)(2,1)S(1)}, u32[]{:S(2)}, u32[]{:S(2)}) collective-permute-start(bf16[1,8,16,256]{3,2,1,0:T(8,128)(2,1)S(1)} %collective-permute-done.4), channel_id=1, source_target_pairs={{0,4},{4,8},{8,12},{12,0},{1,5},{5,9},{9,13},{13,1},{2,6},{6,10},{... | collective-permute-start | bytes 196616 | tf_op jit(solution)/shard_map/ppermute | solution.py:15
  20.1 6.1 %collective-permute-start.6 = (bf16[1,8,16,256]{3,2,1,0:T(8,128)(2,1)S(1)}, bf16[1,8,16,256]{3,2,1,0:T(8,128)(2,1)S(1)}, u32[]{:S(2)}, u32[]{:S(2)}) collective-permute-start(bf16[1,8,16,256]{3,2,1,0:T(8,128)(2,1)S(1)} %collective-permute-done.5), channel_id=1, source_target_pairs={{0,4},{4,8},{8,12},{12,0},{1,5},{5,9},{9,13},{13,1},{2,6},{6,10},{... | collective-permute-start | bytes 196616 | tf_op jit(solution)/shard_map/ppermute | solution.py:15
  28.2 51.2 %copy-start.1 = (f32[1,8,16,256]{3,2,1,0:T(8,128)S(1)}, f32[1,8,16,256]{3,2,1,0:T(8,128)}, u32[]{:S(2)}) copy-start(f32[1,8,16,256]{3,2,1,0:T(8,128)} %param.11) | copy-start | bytes 393220
  28.2 71.6 %copy-start.2 = (f32[8,16,256]{2,1,0:T(8,128)S(1)}, f32[8,16,256]{2,1,0:T(8,128)}, u32[]{:S(2)}) copy-start(f32[8,16,256]{2,1,0:T(8,128)} %param.13) | copy-start | bytes 393220
  28.2 71.6 %copy-start.3 = (f32[1,8,16,256]{3,2,1,0:T(8,128)S(1)}, f32[1,8,16,256]{3,2,1,0:T(8,128)}, u32[]{:S(2)}) copy-start(f32[1,8,16,256]{3,2,1,0:T(8,128)} %param.12) | copy-start | bytes 393220
  78.6 0.8 copy-start
  79.4 6.2 %collective-permute-start = (f32[4,16,256]{2,1,0:T(8,128)S(1)}, f32[4,16,256]{2,1,0:T(8,128)S(1)}, u32[]{:S(2)}, u32[]{:S(2)}) collective-permute-start(f32[4,16,256]{2,1,0:T(8,128)S(1)} %get-tuple-element.171), channel_id=1, source_target_pairs={{4,0},{8,4},{12,8},{5,1},{9,5},{13,9},{6,2},{10,6},{14,10},{7,3},{... | collective-permute-start | bytes 196616 | tf_op jit(solution)/shard_map/ppermute | solution.py:31
  80.7 6.6 %collective-permute-start.1 = (f32[4,16,256]{2,1,0:T(8,128)S(1)}, f32[4,16,256]{2,1,0:T(8,128)S(1)}, u32[]{:S(2)}, u32[]{:S(2)}) collective-permute-start(f32[4,16,256]{2,1,0:T(8,128)S(1)} %get-tuple-element.172), channel_id=1, source_target_pairs={{0,4},{4,8},{8,12},{1,5},{5,9},{9,13},{2,6},{6,10},{10,14},{3,7},{... | collective-permute-start | bytes 196616 | tf_op jit(solution)/shard_map/ppermute | solution.py:29
  87.3 6.2 %collective-permute-start.2 = (f32[16,4,256]{2,1,0:T(4,128)S(1)}, f32[16,4,256]{2,1,0:T(4,128)S(1)}, u32[]{:S(2)}, u32[]{:S(2)}) collective-permute-start(f32[16,4,256]{2,1,0:T(4,128)S(1)} %get-tuple-element.170), channel_id=1, source_target_pairs={{2,0},{3,1},{6,4},{7,5},{10,8},{11,9},{14,12},{15,13},{18,16},{19,... | collective-permute-start | bytes 196616 | tf_op jit(solution)/shard_map/ppermute | solution.py:31
  88.6 6.4 %collective-permute-start.3 = (f32[16,4,256]{2,1,0:T(4,128)S(1)}, f32[16,4,256]{2,1,0:T(4,128)S(1)}, u32[]{:S(2)}, u32[]{:S(2)}) collective-permute-start(f32[16,4,256]{2,1,0:T(4,128)S(1)} %get-tuple-element.169), channel_id=1, source_target_pairs={{0,2},{1,3},{4,6},{5,7},{8,10},{9,11},{12,14},{13,15},{16,18},{17,... | collective-permute-start | bytes 196616 | tf_op jit(solution)/shard_map/ppermute | solution.py:29
Sparse Core Ops, SparseCore 0:
  79.5 20.2 reduce-scatter.1
